TPU v7x, 256 devices: a whole 4x4x8 slice. The times are simulated.
256 devices in a mesh: shard: 16 (over z, core), tensor: 4 (over x), section: 4 (over y).
Axes of the slice: x: 4, y: 4, z: 8, core: 2. Of those that a mesh axis runs over, the one named last changes fastest.
Arguments:
- gradient: bfloat16 [6, 2048, 8192], P(None, ('tensor', 'section'), 'shard'), may hold values from -6 to 6
- basis: bfloat16 [6, 2048, 256], P(None, ('tensor', 'section')), may hold values from -6 to 6
- moment_m: float32 [6, 8192, 256], P(None, ('shard', 'tensor', 'section')), may hold values from -4 to 4
- moment_v: float32 [6, 8192, 256], P(None, ('shard', 'tensor', 'section')), may hold values from 0.002 to 0.02
Outputs:
- delta: bfloat16 [6, 2048, 8192], P(None, ('tensor', 'section'), 'shard')
- basis_new: bfloat16 [6, 2048, 256], P(None, ('tensor', 'section'))
- moment_m_new: float32 [6, 8192, 256], P(None, ('shard', 'tensor', 'section'))
- moment_v_new: float32 [6, 8192, 256], P(None, ('shard', 'tensor', 'section'))
All inputs are finite; a program needn't handle non-finite values. Where the computation divides by a largest or mean magnitude, that divisor is 1e-20 or more.
Results may differ from a plain program's by a relative error of at most 0.0049.
Values may be sent and summed in bfloat16 or wider, within the bound.
A program may use at most 64 MiB of HBM per device.

v0:
```python
import math

import jax
import jax.numpy as jnp
from jax import lax
from jax.sharding import PartitionSpec as P

D = 2048
NS_ITERS = 4


beta_one = 0.9
beta_two = 0.999
bias_one = 1.0 - 0.9**10
bias_two = 1.0 - 0.999**10
eps_adam = 1e-08
galore_gain = 4.0


def gram_total(iterate):
    local_gram = jnp.einsum("kmr,kms->krs", iterate, iterate, precision=lax.Precision.HIGHEST)
    return lax.psum(local_gram, ("tensor", "section"))


def orthogonal(subspace):
    gram_mat = gram_total(subspace)
    row_bound = jnp.max(jnp.sum(jnp.abs(gram_mat), axis=2), axis=1)[:, None, None] + 1e-06
    iterate = subspace / jnp.sqrt(row_bound)
    gram_mat = gram_mat / row_bound
    identity = jnp.eye(gram_mat.shape[1], dtype=jnp.float32)
    for turn_index in range(NS_ITERS):
        factor = 1.5 * identity - 0.5 * gram_mat
        iterate = jnp.einsum("kmr,krs->kms", iterate, factor, precision=lax.Precision.HIGHEST)
        if turn_index + 1 < NS_ITERS:
            gram_mat = gram_total(iterate)
    return iterate


def per_device(gradient, basis, moment_m, moment_v):
    width_root = math.sqrt(D)
    partial_low = jnp.einsum("kmn,kmr->knr", gradient, basis, preferred_element_type=jnp.float32)
    low_rank = (
        lax.psum_scatter(partial_low, ("tensor", "section"), scatter_dimension=1, tiled=True)
        / width_root
    )
    moment_m_new = beta_one * moment_m + (1.0 - beta_one) * low_rank
    moment_v_new = beta_two * moment_v + (1.0 - beta_two) * low_rank * low_rank
    step_low = (moment_m_new / bias_one / (jnp.sqrt(moment_v_new / bias_two) + eps_adam)).astype(
        jnp.bfloat16
    )
    rough_low = low_rank.astype(jnp.bfloat16)
    step_block, rough_block = (
        lax.all_gather(step_low, ("tensor", "section"), axis=1, tiled=True),
        lax.all_gather(rough_low, ("tensor", "section"), axis=1, tiled=True),
    )
    delta = (
        -galore_gain
        / width_root
        * jnp.einsum("kmr,knr->kmn", basis, step_block, preferred_element_type=jnp.float32)
    ).astype(jnp.bfloat16)
    subspace = jnp.einsum("kmn,knr->kmr", gradient, rough_block, preferred_element_type=jnp.float32)
    whole_sum = lax.psum(subspace, "shard")
    basis_new = (width_root * orthogonal(whole_sum)).astype(jnp.bfloat16)
    return (delta, basis_new, moment_m_new, moment_v_new)


def solution(mesh):
    placed = (
        P(None, ("tensor", "section"), "shard"),
        P(None, ("tensor", "section"), None),
        P(None, ("shard", "tensor", "section"), None),
        P(None, ("shard", "tensor", "section"), None),
    )
    return jax.shard_map(
        per_device,
        mesh=mesh,
        in_specs=placed,
        out_specs=(
            P(None, ("tensor", "section"), "shard"),
            P(None, ("tensor", "section"), None),
            P(None, ("shard", "tensor", "section"), None),
            P(None, ("shard", "tensor", "section"), None),
        ),
        check_vma=False,
    )
```

profile of v0, /device:TPU:1, one launch (start us, length us, event | category | flops | bytes accessed | tf_op | source)
XLA Modules:
  0.0 738.0 jit_solution(1374766177256162602)
XLA Ops:
  7.2 1.1 copy-done
  8.3 3.3 fusion.37
  11.6 83.9 %reduce-scatter.2.cloned.1.call-done = f32[6,32,256]{2,1,0:T(8,128)} async-done(((f32[6,512,256]{2,1,0:T(8,128)}), f32[6,32,256]{2,1,0:T(8,128)}) %reduce-scatter.2.cloned.1.call-update) | async-done | bytes 196624 | tf_op jit(solution)/shard_map/reduce_scatter | solution.py:43
  95.5 1.8 divide_convert_fusion
  97.4 49.6 %all-gather.5.cloned.1.call-done = bf16[6,512,256]{2,1,0:T(8,128)(2,1)} async-done(((bf16[6,32,256]{2,1,0:T(8,128)(2,1)}), bf16[6,512,256]{2,1,0:T(8,128)(2,1)}) %all-gather.5.cloned.1.call-update) | async-done | bytes 1572880 | tf_op jit(solution)/shard_map/all_gather | solution.py:54
  147.0 2.9 convolution_bitcast_fusion
  150.1 112.2 %all-reduce.6.cloned.1.call-done = f32[6,128,256]{1,2,0:T(8,128)} async-done(((f32[6,128,256]{1,2,0:T(8,128)}), f32[6,128,256]{1,2,0:T(8,128)}) %all-reduce.6.cloned.1.call-update) | async-done | bytes 786448 | tf_op jit(solution)/shard_map/psum | solution.py:62
  262.3 3.9 fusion.38
  266.3 98.1 %all-reduce.8.cloned.1.call-done = f32[6,256,256]{2,1,0:T(8,128)} async-done(((f32[6,256,256]{2,1,0:T(8,128)}), f32[6,256,256]{2,1,0:T(8,128)}) %all-reduce.8.cloned.1.call-update) | async-done | bytes 1572880 | tf_op jit(solution)/shard_map/psum | solution.py:22
  364.4 1.7 abs_reduce_fusion
  366.3 3.1 fusion.9
  369.4 2.6 fusion.39
  372.1 98.7 %all-reduce.10.cloned.1.call-done = f32[6,256,256]{2,1,0:T(8,128)} async-done(((f32[6,256,256]{2,1,0:T(8,128)}), f32[6,256,256]{2,1,0:T(8,128)}) %all-reduce.10.cloned.1.call-update) | async-done | bytes 1572880 | tf_op jit(solution)/shard_map/psum | solution.py:22
  470.8 2.6 fusion.6
  473.3 2.6 fusion.40
  476.0 0.7 all-gather.3.cloned.1.call-update
  477.0 97.7 %all-reduce.12.cloned.1.call-done = f32[6,256,256]{2,1,0:T(8,128)} async-done(((f32[6,256,256]{2,1,0:T(8,128)}), f32[6,256,256]{2,1,0:T(8,128)}) %all-reduce.12.cloned.1.call-update) | async-done | bytes 1572880 | tf_op jit(solution)/shard_map/psum | solution.py:22
  574.7 2.6 fusion.3
  577.3 2.6 fusion.41
  579.9 46.3 %all-gather.3.cloned.1.call-done = bf16[6,512,256]{2,1,0:T(8,128)(2,1)} async-done(((bf16[6,32,256]{2,1,0:T(8,128)(2,1)}), bf16[6,512,256]{2,1,0:T(8,128)(2,1)}) %all-gather.3.cloned.1.call-update) | async-done | bytes 1572880 | tf_op jit(solution)/shard_map/all_gather | solution.py:53
  626.2 2.0 fusion.13
  628.2 1.2 copy.15
  629.4 98.5 %all-reduce.14.cloned.1.call-done = f32[6,256,256]{2,1,0:T(8,128)} async-done(((f32[6,256,256]{2,1,0:T(8,128)}), f32[6,256,256]{2,1,0:T(8,128)}) %all-reduce.14.cloned.1.call-update) | async-done | bytes 1572880 | tf_op jit(solution)/shard_map/psum | solution.py:22
  727.9 3.3 fusion.17
  (27 shorter events, 0.8 us)
Async XLA Ops:
  7.2 1.1 copy-start
  7.2 88.3 %reduce-scatter.2.cloned.1.call-start = ((), (), s32[]{:S(2)}) async-start(), calls=%async_computation.1 | async-start | bytes 3342336 | tf_op jit(solution)/shard_map/reduce_scatter | solution.py:43
  11.6 83.9 %copy-start.3 = (f32[6,32,256]{2,1,0:T(8,128)S(1)}, f32[6,32,256]{2,1,0:T(8,128)}, u32[]{:S(2)}) copy-start(f32[6,32,256]{2,1,0:T(8,128)} %param.6) | copy-start | bytes 589828
  11.6 83.9 %copy-start.4 = (f32[6,32,256]{2,1,0:T(8,128)S(1)}, f32[6,32,256]{2,1,0:T(8,128)}, u32[]{:S(2)}) copy-start(f32[6,32,256]{2,1,0:T(8,128)} %param.7) | copy-start | bytes 589828
  11.6 135.5 %all-gather.5.cloned.1.call-start = ((), (), s32[]{:S(2)}) async-start(), calls=%async_computation.3 | async-start | bytes 1671168 | tf_op jit(solution)/shard_map/all_gather | solution.py:54
  97.4 164.9 %all-reduce.6.cloned.1.call-start = ((), (), s32[]{:S(2)}) async-start(), calls=%async_computation.4 | async-start | bytes 1572864 | tf_op jit(solution)/shard_map/psum | solution.py:62
  150.0 214.4 %all-reduce.8.cloned.1.call-start = ((), (), s32[]{:S(2)}) async-start(), calls=%async_computation.5 | async-start | bytes 3145728 | tf_op jit(solution)/shard_map/psum | solution.py:22
  266.2 100.0 %copy-start.1 = (f32[6,128,256]{1,2,0:T(8,128)S(1)}, f32[6,128,256]{1,2,0:T(8,128)}, u32[]{:S(2)}) copy-start(f32[6,128,256]{1,2,0:T(8,128)} %all-reduce.6.cloned.1.call-done) | copy-start | bytes 2359300
  266.3 204.5 %all-reduce.10.cloned.1.call-start = ((), (), s32[]{:S(2)}) async-start(), calls=%async_computation.6 | async-start | bytes 3145728 | tf_op jit(solution)/shard_map/psum | solution.py:22
  372.1 202.6 %all-reduce.12.cloned.1.call-start = ((), (), s32[]{:S(2)}) async-start(), calls=%async_computation.7 | async-start | bytes 3145728 | tf_op jit(solution)/shard_map/psum | solution.py:22
  476.0 150.3 %all-gather.3.cloned.1.call-start = ((), (), s32[]{:S(2)}) async-start(), calls=%async_computation.2 | async-start | bytes 1671168 | tf_op jit(solution)/shard_map/all_gather | solution.py:53
  476.7 251.1 %all-reduce.14.cloned.1.call-start = ((), (), s32[]{:S(2)}) async-start(), calls=%async_computation.8 | async-start | bytes 3145728 | tf_op jit(solution)/shard_map/psum | solution.py:22
  579.9 46.4 %copy-start.2 = (bf16[6,128,256]{2,1,0:T(8,128)(2,1)S(1)}, bf16[6,128,256]{2,1,0:T(8,128)(2,1)}, u32[]{:S(2)}) copy-start(bf16[6,128,256]{2,1,0:T(8,128)(2,1)} %param.5) | copy-start | bytes 1179652
Sparse Core Ops, SparseCore 0:
  11.7 83.7 reduce-scatter.1
  98.6 48.4 all-gather.4
  150.1 112.1 all-reduce.5
  266.4 97.9 all-reduce.7
  372.2 98.5 all-reduce.9
  476.1 98.5 all-reduce.11
  577.8 48.4 all-gather.2
  629.5 98.2 all-reduce.13
where the time goes:
time: 739 us; the launch traced here: 738 us
  waiting for transfers between devices  686 us (93%)
  matrix products  31.6 us (4%)
  between operations  14.2 us (2%)
    psum x4, waiting for transfers between devices, gram_total(): return lax.psum(local_gram, ('tensor', 'section'))  393 us
    psum x1, waiting for transfers between devices, per_device(): whole_sum = lax.psum(subspace, 'shard')  112 us
    reduce_scatter x1, waiting for transfers between devices, per_device(): lax.psum_scatter(partial_low, ('tensor', 'section'), scatter_dimension=1,...  83.9 us
    all_gather x1, waiting for transfers between devices, per_device(): lax.all_gather(rough_low, ('tensor', 'section'), axis=1, tiled=True)  49.6 us
    all_gather x1, waiting for transfers between devices, per_device(): lax.all_gather(step_low, ('tensor', 'section'), axis=1, tiled=True)  46.3 us
  transfers between devices with their start and end apart: 8, of which 8 were waited for; matrix products, arithmetic and copies ran while one was open for 1% of the time, Pallas kernels for 0%

commit v1 on v0

v1 whole, which is shorter than its diff:
```python
import functools
import math

import jax
import jax.numpy as jnp
from jax import lax
from jax.experimental import pallas as pl
from jax.experimental.pallas import tpu as pltpu
from jax.sharding import PartitionSpec as P

D = 2048
NS_ITERS = 4
NMAT = 6
RANK = 256
ROWS = 128
RING = 4
PART = 32
ORDER = (0, 3, 1, 4, 2, 5)

beta_one = 0.9
beta_two = 0.999
bias_one = 1.0 - 0.9**10
bias_two = 1.0 - 0.999**10
eps_adam = 1e-08
galore_gain = 4.0

F32 = jnp.float32
BF16 = jnp.bfloat16
MESH = pl.DeviceIdType.MESH


def dot(a, b, ca, cb):
    return lax.dot_general(a, b, (((ca,), (cb,)), ((), ())), preferred_element_type=F32)


def split(a):
    high = a.astype(BF16)
    return high, (a - high.astype(F32)).astype(BF16)


def dot3(a, b, ca=1, cb=0):
    (ah, al), (bh, bl) = a, b
    return dot(ah, bh, ca, cb) + (dot(ah, bl, ca, cb) + dot(al, bh, ca, cb))


def kernel(
    depth,
    g_hbm,
    b_hbm,
    m_hbm,
    v_hbm,
    delta_hbm,
    basis_hbm,
    m_out_hbm,
    v_out_hbm,
    g_v,
    b_v,
    m_v,
    v_v,
    p_f,
    p_b,
    r1,
    rel1,
    q_f,
    q_b,
    r2,
    rel2,
    rough,
    step,
    t_own,
    t_in,
    u_b,
    d_in,
    s_f,
    gram,
    gram_in,
    gram_all,
    base,
    del_v,
    load_sem,
    store_sem,
    rs_send,
    rs_recv,
    ag_send,
    ag_recv,
    t_send,
    t_recv,
    d_send,
    d_recv,
    gr_send,
    gr_recv,
    ga_send,
    ga_recv,
    f_send,
    f_recv,
    fc_send,
    fc_recv,
):
    shard = lax.axis_index("shard")
    x = lax.axis_index("tensor")
    y = lax.axis_index("section")
    z, core = shard // 2, lax.rem(shard, 2)
    partner = {"shard": z * 2 + (1 - core)}
    places = {"tensor": x, "section": y}

    loads = []
    for k in ORDER:
        pair = (
            pltpu.make_async_copy(g_hbm.at[k], g_v.at[k], load_sem.at[0, k]),
            pltpu.make_async_copy(b_hbm.at[k], b_v.at[k], load_sem.at[1, k]),
        )
        for copy in pair:
            copy.start()
        loads.append(pair)
    moments = (
        pltpu.make_async_copy(m_hbm, m_v, load_sem.at[2, 0]),
        pltpu.make_async_copy(v_hbm, v_v, load_sem.at[2, 1]),
    )
    for copy in moments:
        copy.start()

    barrier = pltpu.get_barrier_semaphore()
    greeted = 0
    for dx in range(RING):
        for dy in range(RING):
            if dx or dy:
                there = {"tensor": lax.rem(x + dx, RING), "section": lax.rem(y + dy, RING)}
                pl.semaphore_signal(barrier, inc=1, device_id=there, device_id_type=MESH)
                greeted += 1
    for dz in range(1, depth):
        there = {"shard": lax.rem(z + dz, depth) * 2 + core}
        pl.semaphore_signal(barrier, inc=1, device_id=there, device_id_type=MESH)
        greeted += 1
    pl.semaphore_signal(barrier, inc=1, device_id=partner, device_id_type=MESH)
    greeted += 1

    def project(k):
        g_copy, b_copy = loads[ORDER.index(k)]
        g_copy.wait()
        b_copy.wait()
        part = dot(g_v[k], b_v[k], 0, 0).reshape(RING, RING, PART, RANK)
        p_f[k] = part
        p_b[k] = part.astype(BF16)

    project(ORDER[0])
    pl.semaphore_wait(barrier, greeted)

    sends = []

    def push(src, dst, send_sem, recv_sem, where):
        copy = pltpu.make_async_remote_copy(
            src_ref=src,
            dst_ref=dst,
            send_sem=send_sem,
            recv_sem=recv_sem,
            device_id=where,
            device_id_type=MESH,
        )
        copy.start()
        return copy

    def ring_of(k, stage):
        name = ("tensor", "section")[(stage + (k >= 3)) % 2]
        at = places[name]
        plus, minus, far = (lax.rem(at + i, RING) for i in (1, 3, 2))
        return name, at, plus, minus, far

    def half(h, size):
        return pl.ds(h * size, size)

    def rs_piece(source, k, stage, at, h):
        if stage == 1:
            return source.at[k, at, half(h, PART // 2)]
        if k < 3:
            return source.at[k, at, half(h, 2)]
        return source.at[k, half(h, 2), at]

    def rs_parts(stage):
        return ((p_f, p_b, r1, rel1), (q_f, q_b, r2, rel2))[stage]

    def rs_push(k, stage, src, slot, to):
        name = ring_of(k, stage)[0]
        landing = rs_parts(stage)[2]
        return push(
            src, landing.at[k, slot], rs_send.at[stage, k, slot], rs_recv.at[stage, k, slot], {name: to}
        )

    def rs_start(k, stage):
        name, at, plus, minus, far = ring_of(k, stage)
        source = rs_parts(stage)[1]
        copies = {}
        for slot, to_at, h, to in ((0, far, 0, plus), (1, far, 1, minus), (2, plus, 1, plus), (3, minus, 0, minus)):
            copies[slot] = rs_push(k, stage, rs_piece(source, k, stage, to_at, h), slot, to)
        sends.extend(copies.values())
        return copies

    def rs_relay(k, stage, copies):
        name, at, plus, minus, far = ring_of(k, stage)
        exact, _, landing, relay = rs_parts(stage)
        for slot, h, to in ((0, 0, plus), (1, 1, minus)):
            copies[slot].wait_recv()
            own = rs_piece(exact, k, stage, to, h)[...]
            relay[k, slot] = (own + landing[k, slot].astype(F32)).astype(BF16)
            copies[slot + 4] = rs_push(k, stage, relay.at[k, slot], slot + 4, to)
            sends.append(copies[slot + 4])

    def rs_finish(k, stage, copies):
        name, at, plus, minus, far = ring_of(k, stage)
        exact, _, landing, _ = rs_parts(stage)
        totals = []
        for h, slots in ((0, (3, 4)), (1, (2, 5))):
            total = rs_piece(exact, k, stage, at, h)[...]
            for slot in slots:
                copies[slot].wait_recv()
                total = total + landing[k, slot].astype(F32)
            totals.append(total)
        return totals

    flight = {ORDER[0]: rs_start(ORDER[0], 0)}
    for k in ORDER[1:]:
        project(k)
        flight[k] = rs_start(k, 0)
    for k in ORDER:
        rs_relay(k, 0, flight[k])
    later = {}
    for k in ORDER:
        for h, total in enumerate(rs_finish(k, 0, flight[k])):
            q_f[k, 2 * h : 2 * h + 2] = total
            q_b[k, 2 * h : 2 * h + 2] = total.astype(BF16)
        later[k] = rs_start(k, 1)
    for k in ORDER:
        rs_relay(k, 1, later[k])

    def ag_piece(held, k, stage, at, h):
        if stage == 0:
            if k < 3:
                return held.at[k, x, at, half(h, PART // 2)]
            return held.at[k, at, y, half(h, PART // 2)]
        if k < 3:
            return held.at[k, at, half(h, 2)]
        return held.at[k, half(h, 2), at]

    def ag_push(held, kind, k, stage, at, h, slot, to):
        name = ring_of(k, 1 - stage)[0]
        piece = ag_piece(held, k, stage, at, h)
        copy = push(piece, piece, ag_send.at[kind, stage, k, slot], ag_recv.at[kind, stage, k, slot], {name: to})
        sends.append(copy)
        return copy

    def ag_start(held, kind, k, stage):
        name, at, plus, minus, far = ring_of(k, 1 - stage)
        return {
            slot: ag_push(held, kind, k, stage, at, h, slot, to)
            for slot, h, to in ((0, 0, plus), (3, 1, minus), (1, 1, plus), (2, 0, minus))
        }

    def ag_relay(held, kind, k, stage, copies):
        name, at, plus, minus, far = ring_of(k, 1 - stage)
        copies[0].wait_recv()
        copies[4] = ag_push(held, kind, k, stage, minus, 0, 4, plus)
        copies[3].wait_recv()
        copies[5] = ag_push(held, kind, k, stage, plus, 1, 5, minus)

    def ag_finish(copies):
        for slot in (1, 2, 4, 5):
            copies[slot].wait_recv()

    for copy in moments:
        copy.wait()
    stores = []

    def store(src, dst, sem):
        copy = pltpu.make_async_copy(src, dst, sem)
        copy.start()
        stores.append(copy)

    gather = {}
    for k in ORDER:
        low = jnp.concatenate(rs_finish(k, 1, later[k]), axis=0) * (1.0 / math.sqrt(D))
        rough[k, x, y] = low.astype(BF16)
        gather[k] = ag_start(rough, 0, k, 0)
        first = beta_one * m_v[k] + (1.0 - beta_one) * low
        second = beta_two * v_v[k] + (1.0 - beta_two) * low * low
        m_v[k] = first
        v_v[k] = second
        step[k, x, y] = (first / bias_one / (jnp.sqrt(second / bias_two) + eps_adam)).astype(BF16)
    store(m_v, m_out_hbm, store_sem.at[2, 0])
    store(v_v, v_out_hbm, store_sem.at[2, 1])

    for k in ORDER:
        ag_relay(rough, 0, k, 0, gather[k])
    wide = {}
    for k in ORDER:
        ag_finish(gather[k])
        wide[k] = ag_start(rough, 0, k, 1)
    for k in ORDER:
        ag_relay(rough, 0, k, 1, wide[k])
    walk = {k: ag_start(step, 1, k, 0) for k in ORDER}

    def core_copy(k):
        return pltpu.make_async_remote_copy(
            src_ref=t_own.at[k],
            dst_ref=t_in.at[k],
            send_sem=t_send.at[k],
            recv_sem=t_recv.at[k],
            device_id=partner,
            device_id_type=MESH,
        )

    for k in ORDER:
        ag_finish(wide[k])
        t_own[k] = dot(g_v[k], rough[k].reshape(RING * RING * PART, RANK), 1, 0)

        @pl.when(core != k % 2)
        def _():
            core_copy(k).start()

    for k in ORDER:
        ag_relay(step, 1, k, 0, walk[k])

    def plane_copy(k):
        return pltpu.make_async_remote_copy(
            src_ref=u_b.at[k],
            dst_ref=d_in.at[z],
            send_sem=d_send.at[k],
            recv_sem=d_recv.at[z],
            device_id={"shard": 2 * k + k % 2},
            device_id_type=MESH,
        )

    for k in ORDER:

        @pl.when(core == k % 2)
        def _():
            core_copy(k).wait_recv()
            both = t_own[k] + t_in[k]

            @pl.when(z == k)
            def _():
                s_f[...] = both

            @pl.when(z != k)
            def _():
                u_b[k] = both.astype(BF16)
                plane_copy(k).start()

    stride = {}
    for k in ORDER:
        ag_finish(walk[k])
        stride[k] = ag_start(step, 1, k, 1)
    for k in ORDER:
        ag_relay(step, 1, k, 1, stride[k])

    def delta(k):
        ag_finish(stride[k])
        product = dot(b_v[k], step[k].reshape(RING * RING * PART, RANK), 1, 1)
        del_v[k] = (-galore_gain / math.sqrt(D) * product).astype(BF16)
        store(del_v.at[k], delta_hbm.at[k], store_sem.at[0, k])

    owner = jnp.logical_and(z < NMAT, core == lax.rem(z, 2))
    chunk = RANK // (RING * RING)
    mine = pl.ds(pl.multiple_of((x * RING + y) * chunk, chunk), chunk)
    others = [(dx, dy) for dx in (2, 1, 3, 0) for dy in (2, 1, 3, 0) if dx or dy]

    def gram_copy(dx, dy):
        tx, ty = lax.rem(x + dx, RING), lax.rem(y + dy, RING)
        slot = dx * RING + dy
        return pltpu.make_async_remote_copy(
            src_ref=gram.at[pl.ds(pl.multiple_of((tx * RING + ty) * chunk, chunk), chunk)],
            dst_ref=gram_in.at[slot],
            send_sem=gr_send.at[slot],
            recv_sem=gr_recv.at[slot],
            device_id={"tensor": tx, "section": ty},
            device_id_type=MESH,
        )

    def gram_spread(dx, dy):
        slot = dx * RING + dy
        return pltpu.make_async_remote_copy(
            src_ref=gram_all.at[mine],
            dst_ref=gram_all.at[mine],
            send_sem=ga_send.at[slot],
            recv_sem=ga_recv.at[slot],
            device_id={"tensor": lax.rem(x + dx, RING), "section": lax.rem(y + dy, RING)},
            device_id_type=MESH,
        )

    @pl.when(owner)
    def _():
        for source in range(depth):

            @pl.when(z != source)
            def _():
                pltpu.make_async_remote_copy(
                    src_ref=u_b.at[0],
                    dst_ref=d_in.at[source],
                    send_sem=d_send.at[0],
                    recv_sem=d_recv.at[source],
                    device_id=partner,
                    device_id_type=MESH,
                ).wait_recv()
                s_f[...] += d_in[source].astype(F32)

        whole = split(s_f[...])
        gram[...] = dot3(whole, whole, 0, 0)
        for dx, dy in others:
            gram_copy(dx, dy).start()

    for k in ORDER[:3]:
        delta(k)

    @pl.when(owner)
    def _():
        total = gram[mine]
        for dx, dy in others:
            gram_copy(dx, dy).wait_recv()
            total = total + gram_in[dx * RING + dy]
        gram_all[mine] = total
        for dx, dy in others:
            gram_spread(dx, dy).start()

    for k in ORDER[3:]:
        delta(k)

    def basis_copy(dz):
        return pltpu.make_async_remote_copy(
            src_ref=base.at[z],
            dst_ref=base.at[z],
            send_sem=f_send.at[dz],
            recv_sem=f_recv.at[z],
            device_id={"shard": lax.rem(z + dz, depth) * 2 + core},
            device_id_type=MESH,
        )

    def basis_cross(k):
        return pltpu.make_async_remote_copy(
            src_ref=base.at[k],
            dst_ref=base.at[k],
            send_sem=fc_send.at[k],
            recv_sem=fc_recv.at[k],
            device_id=partner,
            device_id_type=MESH,
        )

    @pl.when(owner)
    def _():
        for dx, dy in others:
            gram_spread(dx, dy).wait_recv()
        gram0 = gram_all[...]
        row_sum = jnp.sum(jnp.abs(gram0), axis=1, keepdims=True)
        bound = jnp.max(row_sum, axis=0, keepdims=True) + 1e-06
        iterate = s_f[...] / jnp.sqrt(bound)
        gram_mat = gram0 / bound
        line = lax.broadcasted_iota(jnp.int32, (RANK, RANK), 0)
        column = lax.broadcasted_iota(jnp.int32, (RANK, RANK), 1)
        identity = jnp.where(line == column, 1.5, 0.0).astype(F32)
        for turn in range(NS_ITERS):
            factor = split(identity - 0.5 * gram_mat)
            if turn + 1 < NS_ITERS:
                gram_mat = dot3(split(dot3(split(gram_mat), factor)), factor)
            iterate = dot3(split(iterate), factor)
        base[z] = (math.sqrt(D) * iterate).astype(BF16)
        for dz in (4, 3, 5, 2, 6, 1, 7):
            basis_copy(dz).start()

    for k in range(NMAT):

        @pl.when(core == k % 2)
        def _():
            @pl.when(z != k)
            def _():
                pltpu.make_async_remote_copy(
                    src_ref=base.at[k],
                    dst_ref=base.at[k],
                    send_sem=f_send.at[0],
                    recv_sem=f_recv.at[k],
                    device_id=partner,
                    device_id_type=MESH,
                ).wait_recv()

            basis_cross(k).start()

    for k in range(NMAT):

        @pl.when(core != k % 2)
        def _():
            basis_cross(k).wait_recv()

        store(base.at[k], basis_hbm.at[k], store_sem.at[1, k])

    for copy in sends:
        copy.wait_send()
    for k in range(NMAT):

        @pl.when(core != k % 2)
        def _():
            core_copy(k).wait_send()

        @pl.when(core == k % 2)
        def _():
            basis_cross(k).wait_send()

            @pl.when(z != k)
            def _():
                plane_copy(k).wait_send()

    @pl.when(owner)
    def _():
        for dx, dy in others:
            gram_copy(dx, dy).wait_send()
            gram_spread(dx, dy).wait_send()
        for dz in range(1, depth):
            basis_copy(dz).wait_send()

    for copy in stores:
        copy.wait()


def per_device(depth, gradient, basis, moment_m, moment_v):
    dma = pltpu.SemaphoreType.DMA
    anywhere = pl.BlockSpec(memory_space=pl.ANY)
    shape = jax.ShapeDtypeStruct
    scratch = [
        pltpu.VMEM(gradient.shape, BF16),
        pltpu.VMEM(basis.shape, BF16),
        pltpu.VMEM(moment_m.shape, F32),
        pltpu.VMEM(moment_v.shape, F32),
        pltpu.VMEM((NMAT, RING, RING, PART, RANK), F32),
        pltpu.VMEM((NMAT, RING, RING, PART, RANK), BF16),
        pltpu.VMEM((NMAT, 6, 2, PART, RANK), BF16),
        pltpu.VMEM((NMAT, 2, 2, PART, RANK), BF16),
        pltpu.VMEM((NMAT, RING, PART, RANK), F32),
        pltpu.VMEM((NMAT, RING, PART, RANK), BF16),
        pltpu.VMEM((NMAT, 6, PART // 2, RANK), BF16),
        pltpu.VMEM((NMAT, 2, PART // 2, RANK), BF16),
        pltpu.VMEM((NMAT, RING, RING, PART, RANK), BF16),
        pltpu.VMEM((NMAT, RING, RING, PART, RANK), BF16),
        pltpu.VMEM((NMAT, ROWS, RANK), F32),
        pltpu.VMEM((NMAT, ROWS, RANK), F32),
        pltpu.VMEM((NMAT, ROWS, RANK), BF16),
        pltpu.VMEM((depth, ROWS, RANK), BF16),
        pltpu.VMEM((ROWS, RANK), F32),
        pltpu.VMEM((RANK, RANK), F32),
        pltpu.VMEM((RING * RING, RANK // (RING * RING), RANK), F32),
        pltpu.VMEM((RANK, RANK), F32),
        pltpu.VMEM((NMAT, ROWS, RANK), BF16),
        pltpu.VMEM(gradient.shape, BF16),
        dma((3, NMAT)),
        dma((3, NMAT)),
        dma((2, NMAT, 6)),
        dma((2, NMAT, 6)),
        dma((2, 2, NMAT, 6)),
        dma((2, 2, NMAT, 6)),
        dma((NMAT,)),
        dma((NMAT,)),
        dma((NMAT,)),
        dma((depth,)),
        dma((RING * RING,)),
        dma((RING * RING,)),
        dma((RING * RING,)),
        dma((RING * RING,)),
        dma((depth,)),
        dma((NMAT,)),
        dma((NMAT,)),
        dma((NMAT,)),
    ]
    return pl.pallas_call(
        functools.partial(kernel, depth),
        out_shape=(
            shape(gradient.shape, BF16),
            shape(basis.shape, BF16),
            shape(moment_m.shape, F32),
            shape(moment_v.shape, F32),
        ),
        in_specs=[anywhere] * 4,
        out_specs=(anywhere,) * 4,
        scratch_shapes=scratch,
        compiler_params=pltpu.CompilerParams(
            collective_id=0, has_side_effects=True, vmem_limit_bytes=48 * 1024 * 1024
        ),
        name="galore_step",
    )(gradient, basis, moment_m, moment_v)


def solution(mesh):
    placed = (
        P(None, ("tensor", "section"), "shard"),
        P(None, ("tensor", "section"), None),
        P(None, ("shard", "tensor", "section"), None),
        P(None, ("shard", "tensor", "section"), None),
    )
    return jax.shard_map(
        functools.partial(per_device, mesh.shape["shard"] // 2),
        mesh=mesh,
        in_specs=placed,
        out_specs=placed,
        check_vma=False,
    )
```

time: 739 us -> 86 us (0.12)
  waiting for transfers between devices: 686 us -> 0 us
  Pallas kernels: 0 us -> 78.2 us
  matrix products: 31.6 us -> 0 us
  between operations: 14.2 us -> 0.65 us
    psum x5 -> x0, waiting for transfers between devices: 505 us -> none  [the longest x4 393 us: gram_total(): return lax.psum(local_gram, ('tensor', 'section'))]
    all_gather x2 -> x0, waiting for transfers between devices: 96 us -> none  [the longest x1 49.6 us: per_device(): lax.all_gather(rough_low, ('tensor', 'section'), axis=1, tiled=True)]
    reduce_scatter x1 -> x0, waiting for transfers between devices: 83.9 us -> none  [per_device(): lax.psum_scatter(partial_low, ('tensor', 'section'), scatter_dimension=1,...]
    pallas_call x0 -> x1, Pallas kernels: none -> 78.2 us  [per_device(): pl.pallas_call(functools.partial(kernel, depth), out_shape=(shape(gradien...]
    dot_general x11 -> x0, matrix products: 31.6 us -> none  [the longest x4 11.8 us: gram_total(): jnp.einsum('kmr,kms->krs', iterate, iterate, precision=lax.Precision.HIGH...]
  transfers between devices with their start and end apart: 8 -> 0, of which waited for: 8 -> 0; matrix products, arithmetic and copies ran while one was open for 1% -> 0% of each run, Pallas kernels for 0% -> 0%
where the time goes in v1:
time: 86 us; the launch traced here: 85.8 us
  Pallas kernels  78.2 us (91%)
  local copies, waits for them, and re-layouts  6.95 us (8%)
    pallas_call x1, Pallas kernels, per_device(): pl.pallas_call(functools.partial(kernel, depth), out_shape=(shape(gradien...  78.2 us
    unnamed x12, local copies, waits for them, and re-layouts  6.95 us

profile of v1, /device:TPU:1, one launch (start us, length us, event | category | flops | bytes accessed | tf_op | source)
XLA Modules:
  0.0 85.8 jit_solution(5673661119479456103)
XLA Ops:
  0.6 0.0 copy-start
  0.6 1.1 %copy-done = bf16[6,128,512]{2,1,0:T(8,128)(2,1)S(1)} copy-done((bf16[6,128,512]{2,1,0:T(8,128)(2,1)S(1)}, bf16[6,128,512]{2,1,0:T(8,128)(2,1)}, u32[]{:S(2)}) %copy-start) | copy-done | bytes 786456
  1.8 0.0 copy-start.1
  1.8 1.0 %copy-done.1 = bf16[6,128,256]{2,1,0:T(8,128)(2,1)S(1)} copy-done((bf16[6,128,256]{2,1,0:T(8,128)(2,1)S(1)}, bf16[6,128,256]{2,1,0:T(8,128)(2,1)}, u32[]{:S(2)}) %copy-start.1) | copy-done | bytes 393240
  2.8 0.0 copy-start.2
  2.8 0.9 %copy-done.2 = f32[6,32,256]{2,1,0:T(8,128)S(1)} copy-done((f32[6,32,256]{2,1,0:T(8,128)S(1)}, f32[6,32,256]{2,1,0:T(8,128)}, u32[]{:S(2)}) %copy-start.2) | copy-done | bytes 196632
  3.7 0.0 copy-start.3
  3.7 0.9 %copy-done.3 = f32[6,32,256]{2,1,0:T(8,128)S(1)} copy-done((f32[6,32,256]{2,1,0:T(8,128)S(1)}, f32[6,32,256]{2,1,0:T(8,128)}, u32[]{:S(2)}) %copy-start.3) | copy-done | bytes 196632
  4.6 78.2 %galore_step.1 = (bf16[6,128,512]{2,1,0:T(8,128)(2,1)S(1)}, bf16[6,128,256]{2,1,0:T(8,128)(2,1)S(1)}, f32[6,32,256]{2,1,0:T(8,128)S(1)}, f32[6,32,256]{2,1,0:T(8,128)S(1)}) custom-call(bf16[6,128,512]{2,1,0:T(8,128)(2,1)S(1)} %copy-done, bf16[6,128,256]{2,1,0:T(8,128)(2,1)S(1)} %copy-done.1, f32[6,32,256]{2,1,0:T(8,128)S(1)} %copy-done.2, ...), custom_call_target="tpu_custom_call" | custom-call | tf_op jit(solution)/shard_map/galore_step/pallas_call | solution.py:567
  82.8 0.9 %copy.12 = bf16[6,128,512]{2,1,0:T(8,128)(2,1)} copy(bf16[6,128,512]{2,1,0:T(8,128)(2,1)S(1)} %get-tuple-element.8) | data formatting | bytes 1572864
  83.7 0.7 copy.13
  84.5 0.7 copy.14
  85.2 0.7 copy.15
Async XLA Ops:
  0.6 1.1 %copy-start = (bf16[6,128,512]{2,1,0:T(8,128)(2,1)S(1)}, bf16[6,128,512]{2,1,0:T(8,128)(2,1)}, u32[]{:S(2)}) copy-start(bf16[6,128,512]{2,1,0:T(8,128)(2,1)} %g_hbm.1) | copy-start | bytes 2359300
  1.8 1.0 %copy-start.1 = (bf16[6,128,256]{2,1,0:T(8,128)(2,1)S(1)}, bf16[6,128,256]{2,1,0:T(8,128)(2,1)}, u32[]{:S(2)}) copy-start(bf16[6,128,256]{2,1,0:T(8,128)(2,1)} %b_hbm.1) | copy-start | bytes 1179652
  2.8 0.9 %copy-start.2 = (f32[6,32,256]{2,1,0:T(8,128)S(1)}, f32[6,32,256]{2,1,0:T(8,128)}, u32[]{:S(2)}) copy-start(f32[6,32,256]{2,1,0:T(8,128)} %m_hbm.1) | copy-start | bytes 589828
  3.7 0.9 %copy-start.3 = (f32[6,32,256]{2,1,0:T(8,128)S(1)}, f32[6,32,256]{2,1,0:T(8,128)}, u32[]{:S(2)}) copy-start(f32[6,32,256]{2,1,0:T(8,128)} %v_hbm.1) | copy-start | bytes 589828

commit v2 on v0

v2 whole, which is shorter than its diff:
```python
import functools
import math

import jax
import jax.numpy as jnp
from jax import lax
from jax.experimental import pallas as pl
from jax.experimental.pallas import tpu as pltpu
from jax.sharding import PartitionSpec as P

D = 2048
NS_ITERS = 4
NMAT = 6
RANK = 256
ROWS = 128
RING = 4
PART = 32
SETS = ((0, 3), (1, 4), (2, 5))
LAG = 1

beta_one = 0.9
beta_two = 0.999
bias_one = 1.0 - 0.9**10
bias_two = 1.0 - 0.999**10
eps_adam = 1e-08
galore_gain = 4.0

F32 = jnp.float32
BF16 = jnp.bfloat16
MESH = pl.DeviceIdType.MESH


def dot(a, b, ca, cb):
    return lax.dot_general(a, b, (((ca,), (cb,)), ((), ())), preferred_element_type=F32)


def split(a):
    high = a.astype(BF16)
    return high, (a - high.astype(F32)).astype(BF16)


def dot3(a, b, ca=1, cb=0):
    (ah, al), (bh, bl) = a, b
    return dot(ah, bh, ca, cb) + (dot(ah, bl, ca, cb) + dot(al, bh, ca, cb))


def kernel(
    depth,
    g_hbm,
    b_hbm,
    m_hbm,
    v_hbm,
    delta_out,
    basis_out,
    m_out,
    v_out,
    g_v,
    b_v,
    m_v,
    v_v,
    p_f,
    p_b,
    r1,
    rel1,
    q_f,
    q_b,
    r2,
    rel2,
    rough,
    step,
    t_own,
    t_in,
    u_b,
    d_in,
    s_f,
    gram,
    gram_in,
    gram_all,
    base,
    del_v,
    load_sem,
    store_sem,
    ring_send,
    rs_recv,
    ag_recv,
    t_recv,
    f_recv,
    fc_recv,
    one_sem,
):
    t_send, d_send, d_recv, gr_send, gr_recv, ga_send, ga_recv, f_send, fc_send = (one_sem.at[i] for i in range(9))
    shard = lax.axis_index("shard")
    x = lax.axis_index("tensor")
    y = lax.axis_index("section")
    z, core = shard // 2, lax.rem(shard, 2)
    partner = {"shard": z * 2 + (1 - core)}
    places = {"tensor": x, "section": y}
    owner = jnp.logical_and(z < NMAT, core == lax.rem(z, 2))

    def local(src, dst, sem):
        copy = pltpu.make_async_copy(src, dst, sem)
        copy.start()
        return copy

    def remote(src, dst, send_sem, recv_sem, where):
        return pltpu.make_async_remote_copy(
            src_ref=src,
            dst_ref=dst,
            send_sem=send_sem,
            recv_sem=recv_sem,
            device_id=where,
            device_id_type=MESH,
        )

    def arrived(like, sem):
        remote(like, like, sem, sem, partner).wait_recv()

    def departed(like, sem):
        remote(like, like, sem, sem, partner).wait_send()

    barrier = pltpu.get_barrier_semaphore()
    peers = [
        {"tensor": lax.rem(x + dx, RING), "section": lax.rem(y + dy, RING)}
        for dx in range(RING)
        for dy in range(RING)
        if dx or dy
    ]
    peers += [{"shard": lax.rem(z + dz, depth) * 2 + core} for dz in range(1, depth)]
    peers.append(partner)
    for there in peers:
        pl.semaphore_signal(barrier, inc=1, device_id=there, device_id_type=MESH)

    b_load = local(b_hbm, b_v, load_sem.at[NMAT])
    g_load = {k: local(g_hbm.at[k], g_v.at[k], load_sem.at[k]) for group in SETS for k in group}
    m_load = local(m_hbm, m_v, load_sem.at[NMAT + 1])
    v_load = local(v_hbm, v_v, load_sem.at[NMAT + 2])

    def project(k):
        g_load[k].wait()
        part = dot(g_v[k], b_v[k], 0, 0).reshape(RING, RING, PART, RANK)
        p_f[k] = part
        p_b[k] = part.astype(BF16)

    b_load.wait()
    for k in SETS[0]:
        project(k)
    pl.semaphore_wait(barrier, len(peers))

    def ring_of(k, stage):
        name = ("tensor", "section")[(stage + (k >= 3)) % 2]
        at = places[name]
        plus, minus, far = (lax.rem(at + i, RING) for i in (1, 3, 2))
        return name, at, plus, minus, far

    def half(h, size):
        return pl.ds(h * size, size)

    def rs_piece(source, k, stage, at, h):
        if stage == 1:
            return source.at[k, at, half(h, PART // 2)]
        if k < 3:
            return source.at[k, at, half(h, 2)]
        return source.at[k, half(h, 2), at]

    rs_parts = ((p_f, p_b, r1, rel1), (q_f, q_b, r2, rel2))

    def rs_push(k, stage, src, slot, to):
        sem = rs_recv.at[stage, k % 3, int(slot >= 2)]
        remote(src, rs_parts[stage][2].at[k, slot], ring_send.at[stage], sem, {ring_of(k, stage)[0]: to}).start()

    def rs_start(group, stage):
        source = rs_parts[stage][1]
        for first in (True, False):
            for k in group:
                name, at, plus, minus, far = ring_of(k, stage)
                if first:
                    rs_push(k, stage, rs_piece(source, k, stage, far, 0), 0, plus)
                    rs_push(k, stage, rs_piece(source, k, stage, far, 1), 1, minus)
                else:
                    rs_push(k, stage, rs_piece(source, k, stage, plus, 1), 2, plus)
                    rs_push(k, stage, rs_piece(source, k, stage, minus, 0), 3, minus)

    def rs_relay(group, stage):
        exact, _, landing, relay = rs_parts[stage]
        arrived(landing.at[0, pl.ds(0, 4)], rs_recv.at[stage, group[0] % 3, 0])
        for k in group:
            name, at, plus, minus, far = ring_of(k, stage)
            for slot, to in ((0, plus), (1, minus)):
                own = rs_piece(exact, k, stage, to, slot)[...]
                relay[k, slot] = (own + landing[k, slot].astype(F32)).astype(BF16)
                rs_push(k, stage, relay.at[k, slot], slot + 4, to)

    def rs_finish(group, stage):
        exact, _, landing, _ = rs_parts[stage]
        arrived(landing.at[pl.ds(0, 2), pl.ds(0, 4)], rs_recv.at[stage, group[0] % 3, 1])
        totals = {}
        for k in group:
            at = ring_of(k, stage)[1]
            for h, (one, two) in enumerate(((3, 4), (2, 5))):
                own = rs_piece(exact, k, stage, at, h)[...]
                totals[k, h] = own + (landing[k, one].astype(F32) + landing[k, two].astype(F32))
        return totals

    def ag_piece(held, k, stage, at, h):
        if stage == 0:
            if k < 3:
                return held.at[k, x, at, half(h, PART // 2)]
            return held.at[k, at, y, half(h, PART // 2)]
        if k < 3:
            return held.at[k, at, half(h, 2)]
        return held.at[k, half(h, 2), at]

    def ag_push(held, kind, k, stage, at, h, slot, to):
        piece = ag_piece(held, k, stage, at, h)
        sem = ag_recv.at[kind, stage, k % 3, int(slot not in (0, 3))]
        remote(piece, piece, ring_send.at[2 + 2 * kind + stage], sem, {ring_of(k, 1 - stage)[0]: to}).start()

    def ag_start(held, kind, group, stage):
        for first in (True, False):
            for k in group:
                name, at, plus, minus, far = ring_of(k, 1 - stage)
                for slot, h, to in ((0, 0, plus), (3, 1, minus)) if first else ((1, 1, plus), (2, 0, minus)):
                    ag_push(held, kind, k, stage, at, h, slot, to)

    def ag_like(stage, pieces):
        landing = (r2, r1)[stage]
        return landing.at[0, pl.ds(0, 4)] if pieces == 4 else landing.at[pl.ds(0, 2), pl.ds(0, 4)]

    def ag_relay(held, kind, group, stage):
        arrived(ag_like(stage, 4), ag_recv.at[kind, stage, group[0] % 3, 0])
        for k in group:
            name, at, plus, minus, far = ring_of(k, 1 - stage)
            ag_push(held, kind, k, stage, minus, 0, 4, plus)
            ag_push(held, kind, k, stage, plus, 1, 5, minus)

    def ag_finish(kind, group, stage):
        arrived(ag_like(stage, 8), ag_recv.at[kind, stage, group[0] % 3, 1])

    def core_copy(k):
        return remote(t_own.at[k], t_in.at[k], t_send, t_recv.at[k % 3], partner)

    def plane_copy(k):
        slot = lax.rem(z - k + depth, depth)
        return remote(u_b.at[k], d_in.at[slot], d_send, d_recv, {"shard": 2 * k + k % 2})

    def begin(group):
        if group != SETS[0]:
            for k in group:
                project(k)
        rs_start(group, 0)

    def turn(group):
        for (k, h), total in rs_finish(group, 0).items():
            q_f[k, 2 * h : 2 * h + 2] = total
            q_b[k, 2 * h : 2 * h + 2] = total.astype(BF16)
        rs_start(group, 1)

    def settle(group):
        if group == SETS[0]:
            m_load.wait()
            v_load.wait()
        totals = rs_finish(group, 1)
        lows = {}
        for k in group:
            lows[k] = jnp.concatenate([totals[k, 0], totals[k, 1]], axis=0) * (1.0 / math.sqrt(D))
            rough[k, x, y] = lows[k].astype(BF16)
        ag_start(rough, 0, group, 0)
        for k in group:
            first = beta_one * m_v[k] + (1.0 - beta_one) * lows[k]
            second = beta_two * v_v[k] + (1.0 - beta_two) * lows[k] * lows[k]
            m_v[k] = first
            v_v[k] = second
            step[k, x, y] = (first / bias_one / (jnp.sqrt(second / bias_two) + eps_adam)).astype(BF16)

    def widen(group):
        ag_finish(0, group, 0)
        ag_start(rough, 0, group, 1)
        ag_start(step, 1, group, 0)

    def multiply(group):
        ag_finish(0, group, 1)
        for k in group:
            t_own[k] = dot(g_v[k], rough[k].reshape(RING * RING * PART, RANK), 1, 0)

            @pl.when(core != k % 2)
            def _():
                core_copy(k).start()

        ag_relay(step, 1, group, 0)

    def scatter(group):
        for k in group:

            @pl.when(core == k % 2)
            def _():
                arrived(t_in.at[k], t_recv.at[k % 3])
                both = t_own[k] + t_in[k]

                @pl.when(z == k)
                def _():
                    s_f[...] = both

                @pl.when(z != k)
                def _():
                    u_b[k] = both.astype(BF16)
                    plane_copy(k).start()

    steps = (
        begin,
        lambda group: rs_relay(group, 0),
        turn,
        lambda group: rs_relay(group, 1),
        settle,
        lambda group: ag_relay(rough, 0, group, 0),
        widen,
        lambda group: ag_relay(rough, 0, group, 1),
        multiply,
        scatter,
    )
    for slot in range(len(steps) + LAG * (len(SETS) - 1)):
        for index in reversed(range(len(SETS))):
            if 0 <= slot - LAG * index < len(steps):
                steps[slot - LAG * index](SETS[index])

    stores = [local(m_v, m_out, store_sem.at[0]), local(v_v, v_out, store_sem.at[1])]
    for group in SETS:
        ag_finish(1, group, 0)
        ag_start(step, 1, group, 1)

    chunk = RANK // (RING * RING)
    mine = pl.ds(pl.multiple_of((x * RING + y) * chunk, chunk), chunk)
    others = [(dx, dy) for dx in (2, 1, 3, 0) for dy in (2, 1, 3, 0) if dx or dy]

    @pl.when(owner)
    def _():
        arrived(d_in.at[pl.ds(1, depth - 1)], d_recv)
        total = s_f[...]
        for slot in range(1, depth):
            total = total + d_in[slot].astype(F32)
        s_f[...] = total
        whole = split(total)
        gram[...] = dot3(whole, whole, 0, 0)
        for dx, dy in others:
            tx, ty = lax.rem(x + dx, RING), lax.rem(y + dy, RING)
            theirs = pl.ds(pl.multiple_of((tx * RING + ty) * chunk, chunk), chunk)
            remote(
                gram.at[theirs], gram_in.at[dx * RING + dy], gr_send, gr_recv, {"tensor": tx, "section": ty}
            ).start()

    for group in SETS:
        ag_relay(step, 1, group, 1)

    @pl.when(owner)
    def _():
        arrived(gram_in.at[pl.ds(1, RING * RING - 1)], gr_recv)
        total = gram[mine]
        for slot in range(1, RING * RING):
            total = total + gram_in[slot]
        gram_all[mine] = total
        for dx, dy in others:
            there = {"tensor": lax.rem(x + dx, RING), "section": lax.rem(y + dy, RING)}
            remote(gram_all.at[mine], gram_all.at[mine], ga_send, ga_recv, there).start()

    for group in SETS:
        ag_finish(1, group, 1)
        for k in group:
            product = dot(b_v[k], step[k].reshape(RING * RING * PART, RANK), 1, 1)
            del_v[k] = (-galore_gain / math.sqrt(D) * product).astype(BF16)
    stores.append(local(del_v, delta_out, store_sem.at[2]))

    @pl.when(owner)
    def _():
        arrived(gram_in.at[pl.ds(1, RING * RING - 1)], ga_recv)
        gram0 = gram_all[...]
        row_sum = jnp.sum(jnp.abs(gram0), axis=1, keepdims=True)
        bound = jnp.max(row_sum, axis=0, keepdims=True) + 1e-06
        iterate = s_f[...] / jnp.sqrt(bound)
        gram_mat = gram0 / bound
        line = lax.broadcasted_iota(jnp.int32, (RANK, RANK), 0)
        column = lax.broadcasted_iota(jnp.int32, (RANK, RANK), 1)
        identity = jnp.where(line == column, 1.5, 0.0).astype(F32)
        for turn_index in range(NS_ITERS):
            factor = split(identity - 0.5 * gram_mat)
            if turn_index + 1 < NS_ITERS:
                gram_mat = dot3(split(dot3(split(gram_mat), factor)), factor)
            iterate = dot3(split(iterate), factor)
        base[...] = (math.sqrt(D) * iterate).astype(BF16)
        for dz in (4, 3, 5, 2, 6, 1, 7):
            there = {"shard": lax.rem(z + dz, depth) * 2 + core}
            remote(base, basis_out.at[z], f_send, f_recv.at[z // 2], there).start()
        remote(base, basis_out.at[z], fc_send, fc_recv.at[z // 2], partner).start()
        local(base, basis_out.at[z], store_sem.at[3])

    for k in range(NMAT):

        @pl.when(jnp.logical_and(core == k % 2, z != k))
        def _():
            arrived(basis_out.at[k], f_recv.at[k // 2])
            remote(basis_out.at[k], basis_out.at[k], fc_send, fc_recv.at[k // 2], partner).start()

    for k in range(NMAT):

        @pl.when(core != k % 2)
        def _():
            arrived(basis_out.at[k], fc_recv.at[k // 2])

    for index, like in enumerate((r1, r2, r2, r1, r2, r1)):
        departed(like, ring_send.at[index])
    departed(t_own.at[pl.ds(0, 3)], t_send)

    @pl.when(owner)
    def _():
        departed(u_b.at[pl.ds(0, 2)], d_send)
        departed(gram_in.at[pl.ds(1, RING * RING - 1)], gr_send)
        departed(gram_in.at[pl.ds(1, RING * RING - 1)], ga_send)
        departed(d_in.at[pl.ds(1, depth - 1)], f_send)
        pltpu.make_async_copy(base, basis_out.at[z], store_sem.at[3]).wait()

    @pl.when(jnp.logical_not(owner))
    def _():
        departed(u_b.at[pl.ds(0, 3)], d_send)

    departed(u_b.at[pl.ds(0, 3)], fc_send)
    for copy in stores:
        copy.wait()


def put(*refs):
    sources, targets, sem = refs[:4], refs[4:8], refs[8]
    copies = [pltpu.make_async_copy(a, b, sem.at[i]) for i, (a, b) in enumerate(zip(sources, targets))]
    for copy in copies:
        copy.start()
    for copy in copies:
        copy.wait()


def per_device(depth, gradient, basis, moment_m, moment_v):
    dma = pltpu.SemaphoreType.DMA
    anywhere = pl.BlockSpec(memory_space=pl.ANY)
    shape = jax.ShapeDtypeStruct
    outs = (
        shape(gradient.shape, BF16),
        shape(basis.shape, BF16),
        shape(moment_m.shape, F32),
        shape(moment_v.shape, F32),
    )
    scratch = [
        pltpu.VMEM(gradient.shape, BF16),
        pltpu.VMEM(basis.shape, BF16),
        pltpu.VMEM(moment_m.shape, F32),
        pltpu.VMEM(moment_v.shape, F32),
        pltpu.VMEM((NMAT, RING, RING, PART, RANK), F32),
        pltpu.VMEM((NMAT, RING, RING, PART, RANK), BF16),
        pltpu.VMEM((NMAT, 6, 2, PART, RANK), BF16),
        pltpu.VMEM((NMAT, 2, 2, PART, RANK), BF16),
        pltpu.VMEM((NMAT, RING, PART, RANK), F32),
        pltpu.VMEM((NMAT, RING, PART, RANK), BF16),
        pltpu.VMEM((NMAT, 6, PART // 2, RANK), BF16),
        pltpu.VMEM((NMAT, 2, PART // 2, RANK), BF16),
        pltpu.VMEM((NMAT, RING, RING, PART, RANK), BF16),
        pltpu.VMEM((NMAT, RING, RING, PART, RANK), BF16),
        pltpu.VMEM((NMAT, ROWS, RANK), F32),
        pltpu.VMEM((NMAT, ROWS, RANK), F32),
        pltpu.VMEM((NMAT, ROWS, RANK), BF16),
        pltpu.VMEM((depth, ROWS, RANK), BF16),
        pltpu.VMEM((ROWS, RANK), F32),
        pltpu.VMEM((RANK, RANK), F32),
        pltpu.VMEM((RING * RING, RANK // (RING * RING), RANK), F32),
        pltpu.VMEM((RANK, RANK), F32),
        pltpu.VMEM((ROWS, RANK), BF16),
        pltpu.VMEM(gradient.shape, BF16),
        dma((NMAT + 3,)),
        dma((4,)),
        dma((6,)),
        dma((2, 3, 2)),
        dma((2, 2, 3, 2)),
        dma((3,)),
        dma((3,)),
        dma((3,)),
        dma((9,)),
    ]
    held = [pltpu.with_memory_space_constraint(a, pltpu.HBM) for a in (gradient, basis, moment_m, moment_v)]
    made = pl.pallas_call(
        functools.partial(kernel, depth),
        out_shape=outs,
        in_specs=[anywhere] * 4,
        out_specs=(anywhere,) * 4,
        scratch_shapes=scratch,
        compiler_params=pltpu.CompilerParams(
            collective_id=0, has_side_effects=True, vmem_limit_bytes=40 * 1024 * 1024
        ),
        name="galore_step",
    )(*held)
    return pl.pallas_call(
        put,
        out_shape=outs,
        in_specs=[anywhere] * 4,
        out_specs=(pl.BlockSpec(memory_space=pltpu.HBM),) * 4,
        scratch_shapes=[dma((4,))],
        compiler_params=pltpu.CompilerParams(vmem_limit_bytes=16 * 1024 * 1024),
        name="put",
    )(*made)


def solution(mesh):
    placed = (
        P(None, ("tensor", "section"), "shard"),
        P(None, ("tensor", "section"), None),
        P(None, ("shard", "tensor", "section"), None),
        P(None, ("shard", "tensor", "section"), None),
    )
    return jax.shard_map(
        functools.partial(per_device, mesh.shape["shard"] // 2),
        mesh=mesh,
        in_specs=placed,
        out_specs=placed,
        check_vma=False,
    )
```

time: 739 us -> 72.9 us (0.10)
  waiting for transfers between devices: 686 us -> 0 us
  Pallas kernels: 0 us -> 72.2 us
  matrix products: 31.6 us -> 0 us
  between operations: 14.2 us -> 0.64 us
    psum x5 -> x0, waiting for transfers between devices: 505 us -> none  [the longest x4 393 us: gram_total(): return lax.psum(local_gram, ('tensor', 'section'))]
    all_gather x2 -> x0, waiting for transfers between devices: 96 us -> none  [the longest x1 49.6 us: per_device(): lax.all_gather(rough_low, ('tensor', 'section'), axis=1, tiled=True)]
    reduce_scatter x1 -> x0, waiting for transfers between devices: 83.9 us -> none  [per_device(): lax.psum_scatter(partial_low, ('tensor', 'section'), scatter_dimension=1,...]
    pallas_call x0 -> x2, Pallas kernels: none -> 72.2 us  [the longest x1 71 us: per_device(): pl.pallas_call(functools.partial(kernel, depth), out_shape=outs, in_specs...]
    dot_general x11 -> x0, matrix products: 31.6 us -> none  [the longest x4 11.8 us: gram_total(): jnp.einsum('kmr,kms->krs', iterate, iterate, precision=lax.Precision.HIGH...]
  transfers between devices with their start and end apart: 8 -> 0, of which waited for: 8 -> 0; matrix products, arithmetic and copies ran while one was open for 1% -> 0% of each run, Pallas kernels for 0% -> 0%
where the time goes in v2:
time: 72.9 us; the launch traced here: 72.8 us
  Pallas kernels  72.2 us (99%)
    pallas_call x1, Pallas kernels, per_device(): pl.pallas_call(functools.partial(kernel, depth), out_shape=outs, in_specs...  71 us

profile of v2, /device:TPU:1, one launch (start us, length us, event | category | flops | bytes accessed | tf_op | source)
XLA Modules:
  0.0 72.8 jit_solution(3035267413239294788)
XLA Ops:
  0.6 71.0 %galore_step.1 = (bf16[6,128,512]{2,1,0:T(8,128)(2,1)S(1)}, bf16[6,128,256]{2,1,0:T(8,128)(2,1)S(1)}, f32[6,32,256]{2,1,0:T(8,128)S(1)}, f32[6,32,256]{2,1,0:T(8,128)S(1)}) custom-call(bf16[6,128,512]{2,1,0:T(8,128)(2,1)} %g_hbm.1, bf16[6,128,256]{2,1,0:T(8,128)(2,1)} %b_hbm.1, f32[6,32,256]{2,1,0:T(8,128)} %m_hbm.1, f32[6,32,256]{2,1,0:T(8,128)} %v_hbm.1), custom_call_target="tpu_custom_call" | custom-call | tf_op jit(solution)/shard_map/galore_step/pallas_call | solution.py:483
  71.7 1.2 %put.1 = (bf16[6,128,512]{2,1,0:T(8,128)(2,1)}, bf16[6,128,256]{2,1,0:T(8,128)(2,1)}, f32[6,32,256]{2,1,0:T(8,128)}, f32[6,32,256]{2,1,0:T(8,128)}) custom-call(bf16[6,128,512]{2,1,0:T(8,128)(2,1)S(1)} %get-tuple-element.8.refs_0_, bf16[6,128,256]{2,1,0:T(8,128)(2,1)S(1)} %get-tuple-element.9.refs_1_, f32[6,32,256]{2,1,0:T(8,128)S(1)} %get-tuple-element.10.refs_2_, ...), custom_call_target="tpu_custom_call" | custom-call | tf_op jit(solution)/shard_map/put/pallas_call | solution.py:494

commit v3 on v2

--- a/solution.py
+++ b/solution.py
@@ -16,7 +16,6 @@
 RING = 4
 PART = 32
 SETS = ((0, 3), (1, 4), (2, 5))
-LAG = 1
 
 beta_one = 0.9
 beta_two = 0.999
@@ -42,6 +41,10 @@
 def dot3(a, b, ca=1, cb=0):
     (ah, al), (bh, bl) = a, b
     return dot(ah, bh, ca, cb) + (dot(ah, bl, ca, cb) + dot(al, bh, ca, cb))
+
+
+def plane(k):
+    return k + k // 3
 
 
 def kernel(
@@ -65,7 +68,6 @@
     q_f,
     q_b,
     r2,
-    rel2,
     rough,
     step,
     t_own,
@@ -87,6 +89,7 @@
     f_recv,
     fc_recv,
     one_sem,
+    told,
 ):
     t_send, d_send, d_recv, gr_send, gr_recv, ga_send, ga_recv, f_send, fc_send = (one_sem.at[i] for i in range(9))
     shard = lax.axis_index("shard")
@@ -95,7 +98,8 @@
     z, core = shard // 2, lax.rem(shard, 2)
     partner = {"shard": z * 2 + (1 - core)}
     places = {"tensor": x, "section": y}
-    owner = jnp.logical_and(z < NMAT, core == lax.rem(z, 2))
+    matrix = z - z // 4
+    owner = jnp.logical_and(lax.rem(z, 4) != 3, core == lax.rem(matrix, 2))
 
     def local(src, dst, sem):
         copy = pltpu.make_async_copy(src, dst, sem)
@@ -123,9 +127,10 @@
         {"tensor": lax.rem(x + dx, RING), "section": lax.rem(y + dy, RING)}
         for dx in range(RING)
         for dy in range(RING)
-        if dx or dy
+        if (dx == 0) != (dy == 0) and 2 not in (dx, dy)
     ]
-    peers += [{"shard": lax.rem(z + dz, depth) * 2 + core} for dz in range(1, depth)]
+    beside = [{"shard": lax.rem(z + dz, depth) * 2 + core} for dz in (1, depth - 1)]
+    peers += beside
     peers.append(partner)
     for there in peers:
         pl.semaphore_signal(barrier, inc=1, device_id=there, device_id_type=MESH)
@@ -142,9 +147,21 @@
         p_b[k] = part.astype(BF16)
 
     b_load.wait()
-    for k in SETS[0]:
-        project(k)
+    for group in SETS:
+        for k in group:
+            project(k)
     pl.semaphore_wait(barrier, len(peers))
+
+    def tell(turn):
+        for there in beside:
+            pl.semaphore_signal(told.at[turn], inc=1, device_id=there, device_id_type=MESH)
+
+    def hear(turn):
+        pl.semaphore_wait(told.at[turn], len(beside))
+        if turn < 2:
+            tell(turn + 1)
+
+    tell(0)
 
     def ring_of(k, stage):
         name = ("tensor", "section")[(stage + (k >= 3)) % 2]
@@ -155,116 +172,104 @@
     def half(h, size):
         return pl.ds(h * size, size)
 
-    def rs_piece(source, k, stage, at, h):
-        if stage == 1:
-            return source.at[k, at, half(h, PART // 2)]
+    def across(k, stage, landing, sem, sources):
+        name, at, plus, minus, far = ring_of(k, stage)
+        for slot, to in enumerate((far, plus, minus)):
+            remote(sources(to), landing(slot), ring_send.at[sem[0]], sem[1], {name: to}).start()
+
+    def piece(source, k, at, h):
         if k < 3:
             return source.at[k, at, half(h, 2)]
         return source.at[k, half(h, 2), at]
 
-    rs_parts = ((p_f, p_b, r1, rel1), (q_f, q_b, r2, rel2))
-
-    def rs_push(k, stage, src, slot, to):
-        sem = rs_recv.at[stage, k % 3, int(slot >= 2)]
-        remote(src, rs_parts[stage][2].at[k, slot], ring_send.at[stage], sem, {ring_of(k, stage)[0]: to}).start()
-
-    def rs_start(group, stage):
-        source = rs_parts[stage][1]
-        for first in (True, False):
-            for k in group:
-                name, at, plus, minus, far = ring_of(k, stage)
-                if first:
-                    rs_push(k, stage, rs_piece(source, k, stage, far, 0), 0, plus)
-                    rs_push(k, stage, rs_piece(source, k, stage, far, 1), 1, minus)
-                else:
-                    rs_push(k, stage, rs_piece(source, k, stage, plus, 1), 2, plus)
-                    rs_push(k, stage, rs_piece(source, k, stage, minus, 0), 3, minus)
-
-    def rs_relay(group, stage):
-        exact, _, landing, relay = rs_parts[stage]
-        arrived(landing.at[0, pl.ds(0, 4)], rs_recv.at[stage, group[0] % 3, 0])
-        for k in group:
-            name, at, plus, minus, far = ring_of(k, stage)
+    def rs_push(k, src, slot, to):
+        sem = rs_recv.at[k % 3, int(slot >= 2)]
+        remote(src, r1.at[k, slot], ring_send.at[0], sem, {ring_of(k, 0)[0]: to}).start()
+
+    def rs_begin(group):
+        for k in group:
+            name, at, plus, minus, far = ring_of(k, 0)
+            rs_push(k, piece(p_b, k, far, 0), 0, plus)
+            rs_push(k, piece(p_b, k, far, 1), 1, minus)
+
+    def rs_direct(group):
+        for k in group:
+            name, at, plus, minus, far = ring_of(k, 0)
+            rs_push(k, piece(p_b, k, plus, 1), 2, plus)
+            rs_push(k, piece(p_b, k, minus, 0), 3, minus)
+
+    def rs_relay(group):
+        arrived(r1.at[0, pl.ds(0, 4)], rs_recv.at[group[0] % 3, 0])
+        for k in group:
+            name, at, plus, minus, far = ring_of(k, 0)
             for slot, to in ((0, plus), (1, minus)):
-                own = rs_piece(exact, k, stage, to, slot)[...]
-                relay[k, slot] = (own + landing[k, slot].astype(F32)).astype(BF16)
-                rs_push(k, stage, relay.at[k, slot], slot + 4, to)
-
-    def rs_finish(group, stage):
-        exact, _, landing, _ = rs_parts[stage]
-        arrived(landing.at[pl.ds(0, 2), pl.ds(0, 4)], rs_recv.at[stage, group[0] % 3, 1])
-        totals = {}
-        for k in group:
-            at = ring_of(k, stage)[1]
+                own = piece(p_f, k, to, slot)[...]
+                rel1[k, slot] = (own + r1[k, slot].astype(F32)).astype(BF16)
+                rs_push(k, rel1.at[k, slot], slot + 4, to)
+
+    def rs_turn(group):
+        arrived(r1.at[pl.ds(0, 2), pl.ds(0, 4)], rs_recv.at[group[0] % 3, 1])
+        for k in group:
+            at = ring_of(k, 0)[1]
             for h, (one, two) in enumerate(((3, 4), (2, 5))):
-                own = rs_piece(exact, k, stage, at, h)[...]
-                totals[k, h] = own + (landing[k, one].astype(F32) + landing[k, two].astype(F32))
-        return totals
-
-    def ag_piece(held, k, stage, at, h):
-        if stage == 0:
-            if k < 3:
-                return held.at[k, x, at, half(h, PART // 2)]
-            return held.at[k, at, y, half(h, PART // 2)]
-        if k < 3:
-            return held.at[k, at, half(h, 2)]
-        return held.at[k, half(h, 2), at]
-
-    def ag_push(held, kind, k, stage, at, h, slot, to):
-        piece = ag_piece(held, k, stage, at, h)
-        sem = ag_recv.at[kind, stage, k % 3, int(slot not in (0, 3))]
-        remote(piece, piece, ring_send.at[2 + 2 * kind + stage], sem, {ring_of(k, 1 - stage)[0]: to}).start()
-
-    def ag_start(held, kind, group, stage):
-        for first in (True, False):
-            for k in group:
-                name, at, plus, minus, far = ring_of(k, 1 - stage)
-                for slot, h, to in ((0, 0, plus), (3, 1, minus)) if first else ((1, 1, plus), (2, 0, minus)):
-                    ag_push(held, kind, k, stage, at, h, slot, to)
-
-    def ag_like(stage, pieces):
-        landing = (r2, r1)[stage]
-        return landing.at[0, pl.ds(0, 4)] if pieces == 4 else landing.at[pl.ds(0, 2), pl.ds(0, 4)]
-
-    def ag_relay(held, kind, group, stage):
-        arrived(ag_like(stage, 4), ag_recv.at[kind, stage, group[0] % 3, 0])
-        for k in group:
-            name, at, plus, minus, far = ring_of(k, 1 - stage)
-            ag_push(held, kind, k, stage, minus, 0, 4, plus)
-            ag_push(held, kind, k, stage, plus, 1, 5, minus)
-
-    def ag_finish(kind, group, stage):
-        arrived(ag_like(stage, 8), ag_recv.at[kind, stage, group[0] % 3, 1])
+                own = piece(p_f, k, at, h)[...]
+                total = own + (r1[k, one].astype(F32) + r1[k, two].astype(F32))
+                q_f[k, 2 * h : 2 * h + 2] = total
+                q_b[k, 2 * h : 2 * h + 2] = total.astype(BF16)
+            across(k, 1, lambda slot: r2.at[k, slot], (1, rs_recv.at[k % 3, 2]), lambda to: q_b.at[k, to])
+
+    def ag_begin(held, kind, group):
+        for k in group:
+            own = held.at[k, x, y]
+            across(k, 1, lambda slot: own, (2 + 2 * kind, ag_recv.at[kind, k % 3, 2]), lambda to: own)
+
+    def ag_push(held, kind, k, at, h, slot, to):
+        sem = ag_recv.at[kind, k % 3, int(slot not in (0, 3))]
+        part = piece(held, k, at, h)
+        remote(part, part, ring_send.at[3 + 2 * kind], sem, {ring_of(k, 0)[0]: to}).start()
+
+    def ag_turn(held, kind, group):
+        arrived(r2.at[pl.ds(0, 2)], ag_recv.at[kind, group[0] % 3, 2])
+        for k in group:
+            name, at, plus, minus, far = ring_of(k, 0)
+            ag_push(held, kind, k, at, 0, 0, plus)
+            ag_push(held, kind, k, at, 1, 3, minus)
+
+    def ag_direct(held, kind, group):
+        for k in group:
+            name, at, plus, minus, far = ring_of(k, 0)
+            ag_push(held, kind, k, at, 1, 1, plus)
+            ag_push(held, kind, k, at, 0, 2, minus)
+
+    def ag_relay(held, kind, group):
+        arrived(r1.at[0, pl.ds(0, 4)], ag_recv.at[kind, group[0] % 3, 0])
+        for k in group:
+            name, at, plus, minus, far = ring_of(k, 0)
+            ag_push(held, kind, k, minus, 0, 4, plus)
+            ag_push(held, kind, k, plus, 1, 5, minus)
+
+    def ag_finish(kind, group):
+        arrived(r1.at[pl.ds(0, 2), pl.ds(0, 4)], ag_recv.at[kind, group[0] % 3, 1])
 
     def core_copy(k):
         return remote(t_own.at[k], t_in.at[k], t_send, t_recv.at[k % 3], partner)
 
     def plane_copy(k):
-        slot = lax.rem(z - k + depth, depth)
-        return remote(u_b.at[k], d_in.at[slot], d_send, d_recv, {"shard": 2 * k + k % 2})
-
-    def begin(group):
-        if group != SETS[0]:
-            for k in group:
-                project(k)
-        rs_start(group, 0)
-
-    def turn(group):
-        for (k, h), total in rs_finish(group, 0).items():
-            q_f[k, 2 * h : 2 * h + 2] = total
-            q_b[k, 2 * h : 2 * h + 2] = total.astype(BF16)
-        rs_start(group, 1)
+        slot = lax.rem(z - plane(k) + depth, depth)
+        return remote(u_b.at[k], d_in.at[slot], d_send, d_recv, {"shard": 2 * plane(k) + k % 2})
 
     def settle(group):
+        arrived(r2.at[pl.ds(0, 2)], rs_recv.at[group[0] % 3, 2])
+        lows = {}
+        for k in group:
+            own = q_f[k, ring_of(k, 1)[1]]
+            total = own + (r2[k, 0].astype(F32) + r2[k, 1].astype(F32) + r2[k, 2].astype(F32))
+            lows[k] = total * (1.0 / math.sqrt(D))
+            rough[k, x, y] = lows[k].astype(BF16)
+        ag_begin(rough, 0, group)
         if group == SETS[0]:
             m_load.wait()
             v_load.wait()
-        totals = rs_finish(group, 1)
-        lows = {}
-        for k in group:
-            lows[k] = jnp.concatenate([totals[k, 0], totals[k, 1]], axis=0) * (1.0 / math.sqrt(D))
-            rough[k, x, y] = lows[k].astype(BF16)
-        ag_start(rough, 0, group, 0)
         for k in group:
             first = beta_one * m_v[k] + (1.0 - beta_one) * lows[k]
             second = beta_two * v_v[k] + (1.0 - beta_two) * lows[k] * lows[k]
@@ -272,21 +277,14 @@
             v_v[k] = second
             step[k, x, y] = (first / bias_one / (jnp.sqrt(second / bias_two) + eps_adam)).astype(BF16)
 
-    def widen(group):
-        ag_finish(0, group, 0)
-        ag_start(rough, 0, group, 1)
-        ag_start(step, 1, group, 0)
-
     def multiply(group):
-        ag_finish(0, group, 1)
+        ag_finish(0, group)
         for k in group:
             t_own[k] = dot(g_v[k], rough[k].reshape(RING * RING * PART, RANK), 1, 0)
 
             @pl.when(core != k % 2)
             def _():
                 core_copy(k).start()
-
-        ag_relay(step, 1, group, 0)
 
     def scatter(group):
         for k in group:
@@ -296,37 +294,42 @@
                 arrived(t_in.at[k], t_recv.at[k % 3])
                 both = t_own[k] + t_in[k]
 
-                @pl.when(z == k)
+                @pl.when(z == plane(k))
                 def _():
                     s_f[...] = both
 
-                @pl.when(z != k)
+                @pl.when(z != plane(k))
                 def _():
                     u_b[k] = both.astype(BF16)
                     plane_copy(k).start()
 
-    steps = (
-        begin,
-        lambda group: rs_relay(group, 0),
-        turn,
-        lambda group: rs_relay(group, 1),
+    for task in (
+        rs_begin,
+        rs_direct,
+        rs_relay,
+        rs_turn,
         settle,
-        lambda group: ag_relay(rough, 0, group, 0),
-        widen,
-        lambda group: ag_relay(rough, 0, group, 1),
-        multiply,
-        scatter,
-    )
-    for slot in range(len(steps) + LAG * (len(SETS) - 1)):
-        for index in reversed(range(len(SETS))):
-            if 0 <= slot - LAG * index < len(steps):
-                steps[slot - LAG * index](SETS[index])
+        functools.partial(ag_turn, rough, 0),
+        functools.partial(ag_direct, rough, 0),
+        functools.partial(ag_relay, rough, 0),
+        functools.partial(ag_begin, step, 1),
+    ):
+        for group in SETS:
+            task(group)
+        if task in (rs_relay, settle):
+            hear(int(task is settle))
+    hear(2)
+    multiply(SETS[0])
+    multiply(SETS[1])
+    scatter(SETS[0])
+    multiply(SETS[2])
+    scatter(SETS[1])
+    scatter(SETS[2])
+    for task in (functools.partial(ag_turn, step, 1), functools.partial(ag_direct, step, 1)):
+        for group in SETS:
+            task(group)
 
     stores = [local(m_v, m_out, store_sem.at[0]), local(v_v, v_out, store_sem.at[1])]
-    for group in SETS:
-        ag_finish(1, group, 0)
-        ag_start(step, 1, group, 1)
-
     chunk = RANK // (RING * RING)
     mine = pl.ds(pl.multiple_of((x * RING + y) * chunk, chunk), chunk)
     others = [(dx, dy) for dx in (2, 1, 3, 0) for dy in (2, 1, 3, 0) if dx or dy]
@@ -348,7 +351,7 @@
             ).start()
 
     for group in SETS:
-        ag_relay(step, 1, group, 1)
+        ag_relay(step, 1, group)
 
     @pl.when(owner)
     def _():
@@ -362,7 +365,7 @@
             remote(gram_all.at[mine], gram_all.at[mine], ga_send, ga_recv, there).start()
 
     for group in SETS:
-        ag_finish(1, group, 1)
+        ag_finish(1, group)
         for k in group:
             product = dot(b_v[k], step[k].reshape(RING * RING * PART, RANK), 1, 1)
             del_v[k] = (-galore_gain / math.sqrt(D) * product).astype(BF16)
@@ -387,13 +390,13 @@
         base[...] = (math.sqrt(D) * iterate).astype(BF16)
         for dz in (4, 3, 5, 2, 6, 1, 7):
             there = {"shard": lax.rem(z + dz, depth) * 2 + core}
-            remote(base, basis_out.at[z], f_send, f_recv.at[z // 2], there).start()
-        remote(base, basis_out.at[z], fc_send, fc_recv.at[z // 2], partner).start()
-        local(base, basis_out.at[z], store_sem.at[3])
+            remote(base, basis_out.at[matrix], f_send, f_recv.at[matrix // 2], there).start()
+        remote(base, basis_out.at[matrix], fc_send, fc_recv.at[matrix // 2], partner).start()
+        local(base, basis_out.at[matrix], store_sem.at[3])
 
     for k in range(NMAT):
 
-        @pl.when(jnp.logical_and(core == k % 2, z != k))
+        @pl.when(jnp.logical_and(core == k % 2, z != plane(k)))
         def _():
             arrived(basis_out.at[k], f_recv.at[k // 2])
             remote(basis_out.at[k], basis_out.at[k], fc_send, fc_recv.at[k // 2], partner).start()
@@ -414,7 +417,7 @@
         departed(gram_in.at[pl.ds(1, RING * RING - 1)], gr_send)
         departed(gram_in.at[pl.ds(1, RING * RING - 1)], ga_send)
         departed(d_in.at[pl.ds(1, depth - 1)], f_send)
-        pltpu.make_async_copy(base, basis_out.at[z], store_sem.at[3]).wait()
+        pltpu.make_async_copy(base, basis_out.at[matrix], store_sem.at[3]).wait()
 
     @pl.when(jnp.logical_not(owner))
     def _():
@@ -455,8 +458,7 @@
         pltpu.VMEM((NMAT, 2, 2, PART, RANK), BF16),
         pltpu.VMEM((NMAT, RING, PART, RANK), F32),
         pltpu.VMEM((NMAT, RING, PART, RANK), BF16),
-        pltpu.VMEM((NMAT, 6, PART // 2, RANK), BF16),
-        pltpu.VMEM((NMAT, 2, PART // 2, RANK), BF16),
+        pltpu.VMEM((NMAT, 3, PART, RANK), BF16),
         pltpu.VMEM((NMAT, RING, RING, PART, RANK), BF16),
         pltpu.VMEM((NMAT, RING, RING, PART, RANK), BF16),
         pltpu.VMEM((NMAT, ROWS, RANK), F32),
@@ -472,12 +474,13 @@
         dma((NMAT + 3,)),
         dma((4,)),
         dma((6,)),
-        dma((2, 3, 2)),
-        dma((2, 2, 3, 2)),
+        dma((3, 3)),
+        dma((2, 3, 3)),
         dma((3,)),
         dma((3,)),
         dma((3,)),
         dma((9,)),
+        pltpu.SemaphoreType.REGULAR((3,)),
     ]
     held = [pltpu.with_memory_space_constraint(a, pltpu.HBM) for a in (gradient, basis, moment_m, moment_v)]
     made = pl.pallas_call(

time: 72.9 us -> 66.2 us (0.908)
  Pallas kernels: 72.2 us -> 65.5 us
    pallas_call x1, Pallas kernels: 71 us -> 64.3 us  [per_device(): pl.pallas_call(functools.partial(kernel, depth), out_shape=outs, in_specs...]
where the time goes in v3:
time: 66.2 us; the launch traced here: 66.1 us
  Pallas kernels  65.5 us (99%)
    pallas_call x1, Pallas kernels, per_device(): pl.pallas_call(functools.partial(kernel, depth), out_shape=outs, in_specs...  64.3 us

profile of v3, /device:TPU:1, one launch (start us, length us, event | category | flops | bytes accessed | tf_op | source)
XLA Modules:
  0.0 66.1 jit_solution(9724518428165937944)
XLA Ops:
  0.6 64.3 %galore_step.1 = (bf16[6,128,512]{2,1,0:T(8,128)(2,1)S(1)}, bf16[6,128,256]{2,1,0:T(8,128)(2,1)S(1)}, f32[6,32,256]{2,1,0:T(8,128)S(1)}, f32[6,32,256]{2,1,0:T(8,128)S(1)}) custom-call(bf16[6,128,512]{2,1,0:T(8,128)(2,1)} %g_hbm.1, bf16[6,128,256]{2,1,0:T(8,128)(2,1)} %b_hbm.1, f32[6,32,256]{2,1,0:T(8,128)} %m_hbm.1, f32[6,32,256]{2,1,0:T(8,128)} %v_hbm.1), custom_call_target="tpu_custom_call" | custom-call | tf_op jit(solution)/shard_map/galore_step/pallas_call | solution.py:486
  64.9 1.2 %put.1 = (bf16[6,128,512]{2,1,0:T(8,128)(2,1)}, bf16[6,128,256]{2,1,0:T(8,128)(2,1)}, f32[6,32,256]{2,1,0:T(8,128)}, f32[6,32,256]{2,1,0:T(8,128)}) custom-call(bf16[6,128,512]{2,1,0:T(8,128)(2,1)S(1)} %get-tuple-element.8.refs_0_, bf16[6,128,256]{2,1,0:T(8,128)(2,1)S(1)} %get-tuple-element.9.refs_1_, f32[6,32,256]{2,1,0:T(8,128)S(1)} %get-tuple-element.10.refs_2_, ...), custom_call_target="tpu_custom_call" | custom-call | tf_op jit(solution)/shard_map/put/pallas_call | solution.py:497

commit v4 on v3

--- a/solution.py
+++ b/solution.py
@@ -86,12 +86,13 @@
     rs_recv,
     ag_recv,
     t_recv,
+    f_send,
     f_recv,
     fc_recv,
     one_sem,
     told,
 ):
-    t_send, d_send, d_recv, gr_send, gr_recv, ga_send, ga_recv, f_send, fc_send = (one_sem.at[i] for i in range(9))
+    t_send, d_send, d_recv, gr_send, gr_recv, ga_send, ga_recv, fc_send = (one_sem.at[i] for i in range(8))
     shard = lax.axis_index("shard")
     x = lax.axis_index("tensor")
     y = lax.axis_index("section")
@@ -248,6 +249,18 @@
             ag_push(held, kind, k, minus, 0, 4, plus)
             ag_push(held, kind, k, plus, 1, 5, minus)
 
+    def ag_full(held, kind, group):
+        arrived(r2.at[pl.ds(0, 2)], ag_recv.at[kind, group[0] % 3, 2])
+        for k in group:
+            name, at, plus, minus, far = ring_of(k, 0)
+            for to in (far, plus, minus):
+                for h in range(2):
+                    part = piece(held, k, at, h)
+                    remote(part, part, ring_send.at[3 + 2 * kind], ag_recv.at[kind, k % 3, 1], {name: to}).start()
+
+    def ag_whole(kind, group):
+        arrived(r1.at[pl.ds(0, 2)], ag_recv.at[kind, group[0] % 3, 1])
+
     def ag_finish(kind, group):
         arrived(r1.at[pl.ds(0, 2), pl.ds(0, 4)], ag_recv.at[kind, group[0] % 3, 1])
 
@@ -278,13 +291,19 @@
             step[k, x, y] = (first / bias_one / (jnp.sqrt(second / bias_two) + eps_adam)).astype(BF16)
 
     def multiply(group):
-        ag_finish(0, group)
-        for k in group:
+        ag_whole(0, group)
+
+        def product(k):
             t_own[k] = dot(g_v[k], rough[k].reshape(RING * RING * PART, RANK), 1, 0)
 
-            @pl.when(core != k % 2)
+        for parity in range(2):
+            kept, given = sorted(group, key=lambda k: k % 2 != parity)
+
+            @pl.when(core == parity)
             def _():
-                core_copy(k).start()
+                product(given)
+                core_copy(given).start()
+                product(kept)
 
     def scatter(group):
         for k in group:
@@ -309,9 +328,7 @@
         rs_relay,
         rs_turn,
         settle,
-        functools.partial(ag_turn, rough, 0),
-        functools.partial(ag_direct, rough, 0),
-        functools.partial(ag_relay, rough, 0),
+        functools.partial(ag_full, rough, 0),
         functools.partial(ag_begin, step, 1),
     ):
         for group in SETS:
@@ -319,12 +336,9 @@
         if task in (rs_relay, settle):
             hear(int(task is settle))
     hear(2)
-    multiply(SETS[0])
-    multiply(SETS[1])
-    scatter(SETS[0])
-    multiply(SETS[2])
-    scatter(SETS[1])
-    scatter(SETS[2])
+    for group in SETS:
+        multiply(group)
+        scatter(group)
     for task in (functools.partial(ag_turn, step, 1), functools.partial(ag_direct, step, 1)):
         for group in SETS:
             task(group)
@@ -388,20 +402,36 @@
                 gram_mat = dot3(split(dot3(split(gram_mat), factor)), factor)
             iterate = dot3(split(iterate), factor)
         base[...] = (math.sqrt(D) * iterate).astype(BF16)
-        for dz in (4, 3, 5, 2, 6, 1, 7):
+        for dz in (3, 5, 2, 6, 1, 7):
             there = {"shard": lax.rem(z + dz, depth) * 2 + core}
-            remote(base, basis_out.at[matrix], f_send, f_recv.at[matrix // 2], there).start()
+            remote(base, basis_out.at[matrix], f_send.at[matrix // 2], f_recv.at[matrix // 2], there).start()
         remote(base, basis_out.at[matrix], fc_send, fc_recv.at[matrix // 2], partner).start()
         local(base, basis_out.at[matrix], store_sem.at[3])
 
-    for k in range(NMAT):
-
-        @pl.when(jnp.logical_and(core == k % 2, z != plane(k)))
+    def pass_on(k, offset):
+        for source, target, part in ((3, 4, 0), (5, 4, 1)):
+            if source == offset:
+                rows = pl.ds(0, ROWS) if part is None else half(part, ROWS // 2)
+                there = {"shard": lax.rem(z + (target - source) + depth, depth) * 2 + core}
+                held = basis_out.at[k, rows]
+                remote(held, held, f_send.at[k // 2], f_recv.at[k // 2], there).start()
+
+    ordered = [k for group in SETS for k in group]
+    for k in ordered:
+        offset = lax.rem(z - plane(k) + depth, depth)
+
+        @pl.when(jnp.logical_and(core == k % 2, offset != 0))
         def _():
             arrived(basis_out.at[k], f_recv.at[k // 2])
+            for source in (3, 5):
+
+                @pl.when(offset == source)
+                def _():
+                    pass_on(k, source)
+
             remote(basis_out.at[k], basis_out.at[k], fc_send, fc_recv.at[k // 2], partner).start()
 
-    for k in range(NMAT):
+    for k in ordered:
 
         @pl.when(core != k % 2)
         def _():
@@ -416,12 +446,19 @@
         departed(u_b.at[pl.ds(0, 2)], d_send)
         departed(gram_in.at[pl.ds(1, RING * RING - 1)], gr_send)
         departed(gram_in.at[pl.ds(1, RING * RING - 1)], ga_send)
-        departed(d_in.at[pl.ds(1, depth - 1)], f_send)
+        departed(d_in.at[pl.ds(0, 6)], f_send.at[matrix // 2])
         pltpu.make_async_copy(base, basis_out.at[matrix], store_sem.at[3]).wait()
 
     @pl.when(jnp.logical_not(owner))
     def _():
         departed(u_b.at[pl.ds(0, 3)], d_send)
+
+    for k in range(NMAT):
+        offset = lax.rem(z - plane(k) + depth, depth)
+
+        @pl.when(jnp.logical_and(core == k % 2, jnp.logical_or(offset == 3, offset == 5)))
+        def _():
+            departed(r2.at[0:1, pl.ds(0, 2)], f_send.at[k // 2])
 
     departed(u_b.at[pl.ds(0, 3)], fc_send)
     for copy in stores:
@@ -479,7 +516,8 @@
         dma((3,)),
         dma((3,)),
         dma((3,)),
-        dma((9,)),
+        dma((3,)),
+        dma((8,)),
         pltpu.SemaphoreType.REGULAR((3,)),
     ]
     held = [pltpu.with_memory_space_constraint(a, pltpu.HBM) for a in (gradient, basis, moment_m, moment_v)]

time: 66.2 us -> 65.2 us (0.985); the launches traced: 66.1 us -> 64 us
  Pallas kernels: 65.5 us -> 63.4 us
    pallas_call x1, Pallas kernels: 64.3 us -> 62.2 us  [per_device(): pl.pallas_call(functools.partial(kernel, depth), out_shape=outs, in_specs...]
where the time goes in v4:
time: 65.2 us; the launch traced here: 64 us
  Pallas kernels  63.4 us (97%)
    pallas_call x1, Pallas kernels, per_device(): pl.pallas_call(functools.partial(kernel, depth), out_shape=outs, in_specs...  62.2 us

profile of v4, /device:TPU:1, one launch (start us, length us, event | category | flops | bytes accessed | tf_op | source)
XLA Modules:
  0.0 64.0 jit_solution(8796205794994742692)
XLA Ops:
  0.6 62.2 %galore_step.1 = (bf16[6,128,512]{2,1,0:T(8,128)(2,1)S(1)}, bf16[6,128,256]{2,1,0:T(8,128)(2,1)S(1)}, f32[6,32,256]{2,1,0:T(8,128)S(1)}, f32[6,32,256]{2,1,0:T(8,128)S(1)}) custom-call(bf16[6,128,512]{2,1,0:T(8,128)(2,1)} %g_hbm.1, bf16[6,128,256]{2,1,0:T(8,128)(2,1)} %b_hbm.1, f32[6,32,256]{2,1,0:T(8,128)} %m_hbm.1, f32[6,32,256]{2,1,0:T(8,128)} %v_hbm.1), custom_call_target="tpu_custom_call" | custom-call | tf_op jit(solution)/shard_map/galore_step/pallas_call | solution.py:524
  62.8 1.2 %put.1 = (bf16[6,128,512]{2,1,0:T(8,128)(2,1)}, bf16[6,128,256]{2,1,0:T(8,128)(2,1)}, f32[6,32,256]{2,1,0:T(8,128)}, f32[6,32,256]{2,1,0:T(8,128)}) custom-call(bf16[6,128,512]{2,1,0:T(8,128)(2,1)S(1)} %get-tuple-element.8.refs_0_, bf16[6,128,256]{2,1,0:T(8,128)(2,1)S(1)} %get-tuple-element.9.refs_1_, f32[6,32,256]{2,1,0:T(8,128)S(1)} %get-tuple-element.10.refs_2_, ...), custom_call_target="tpu_custom_call" | custom-call | tf_op jit(solution)/shard_map/put/pallas_call | solution.py:535

commit v5 on v4

--- a/solution.py
+++ b/solution.py
@@ -148,9 +148,8 @@
         p_b[k] = part.astype(BF16)
 
     b_load.wait()
-    for group in SETS:
-        for k in group:
-            project(k)
+    for k in SETS[0]:
+        project(k)
     pl.semaphore_wait(barrier, len(peers))
 
     def tell(turn):
@@ -189,6 +188,8 @@
 
     def rs_begin(group):
         for k in group:
+            if group != SETS[0]:
+                project(k)
             name, at, plus, minus, far = ring_of(k, 0)
             rs_push(k, piece(p_b, k, far, 0), 0, plus)
             rs_push(k, piece(p_b, k, far, 1), 1, minus)

time: 65.2 us -> 64.1 us (0.983)
  no operation moved by 1% of the time
where the time goes in v5:
time: 64.1 us; the launch traced here: 63.4 us
  Pallas kernels  62.8 us (98%)
    pallas_call x1, Pallas kernels, per_device(): pl.pallas_call(functools.partial(kernel, depth), out_shape=outs, in_specs...  61.6 us

profile of v5, /device:TPU:1, one launch (start us, length us, event | category | flops | bytes accessed | tf_op | source)
XLA Modules:
  0.0 63.4 jit_solution(8813525734686315031)
XLA Ops:
  0.6 61.6 %galore_step.1 = (bf16[6,128,512]{2,1,0:T(8,128)(2,1)S(1)}, bf16[6,128,256]{2,1,0:T(8,128)(2,1)S(1)}, f32[6,32,256]{2,1,0:T(8,128)S(1)}, f32[6,32,256]{2,1,0:T(8,128)S(1)}) custom-call(bf16[6,128,512]{2,1,0:T(8,128)(2,1)} %g_hbm.1, bf16[6,128,256]{2,1,0:T(8,128)(2,1)} %b_hbm.1, f32[6,32,256]{2,1,0:T(8,128)} %m_hbm.1, f32[6,32,256]{2,1,0:T(8,128)} %v_hbm.1), custom_call_target="tpu_custom_call" | custom-call | tf_op jit(solution)/shard_map/galore_step/pallas_call | solution.py:525
  62.3 1.2 %put.1 = (bf16[6,128,512]{2,1,0:T(8,128)(2,1)}, bf16[6,128,256]{2,1,0:T(8,128)(2,1)}, f32[6,32,256]{2,1,0:T(8,128)}, f32[6,32,256]{2,1,0:T(8,128)}) custom-call(bf16[6,128,512]{2,1,0:T(8,128)(2,1)S(1)} %get-tuple-element.8.refs_0_, bf16[6,128,256]{2,1,0:T(8,128)(2,1)S(1)} %get-tuple-element.9.refs_1_, f32[6,32,256]{2,1,0:T(8,128)S(1)} %get-tuple-element.10.refs_2_, ...), custom_call_target="tpu_custom_call" | custom-call | tf_op jit(solution)/shard_map/put/pallas_call | solution.py:536
